TPU v7x, 512 devices: a whole 4x4x16 slice. The times are simulated.
512 devices in a mesh: tile: 128 (over z, x, core), lev: 4 (over y).
Axes of the slice: x: 4, y: 4, z: 16, core: 2. Of those that a mesh axis runs over, the one named last changes fastest.
Arguments:
- probes: bfloat16 [512, 32, 8, 128], P('tile', None, 'lev'), may hold values from -1 to 1, as said below
- stddev: float32 [512, 32, 128], P('tile'), may hold values from 0.5 to 2
- diffusivity: float32 [128], replicated, may hold values from 0.03 to 0.24
- counts: int32 [128, 128], P('tile'), may hold values from 0 to 16, as said below
- columns: int32 [128, 128, 16], P('tile'), may hold values from 0 to 127
- jacobian: bfloat16 [128, 256, 32], P('tile'), may hold values from -1 to 1
- offsets: int32 [128, 256], replicated, may hold values from 0 to 96
- obs_weights: float32 [128, 256], replicated, may hold values from 0.25 to 4
Outputs:
- hessian_probe: float32 [512, 32, 8, 128], P('tile', None, 'lev')
- trace_share: float32 [128], P('tile')
Inputs may be any that keep to these rules, and one draw needn't show every extreme that they name: `counts`: in every draw one section receives 16 observations from every tile. `columns`: slots at or past counts[t,d] are unused. `probes`: each entry is +1 or -1.
All inputs are finite; a program needn't handle non-finite values.
Results may differ from a plain program's by a relative error of at most 0.00045.
The roundings to bfloat16 on the way count: a program that leaves them out, or rounds other values in their place, can miss the bound.
Values may be sent and summed in bfloat16 or wider, within the bound.
No kernel may reach another device: no remote copies, remote signals or barrier semaphores. Data moves between devices by JAX's collectives and lax.ppermute only.
A program may use at most 64 MiB of HBM per device.

v0:
```python
import math
import jax
import jax.numpy as jnp
from jax import lax
from jax.sharding import PartitionSpec as P

LEV = 128
CH = 256
PROBES = 8
NSTEP = 2


def padded_2(cells, sides, width):
    for axis, dim in sides:
        count = lax.axis_size(axis)
        head = lax.slice_in_dim(cells, 0, width, axis=dim)
        tail = lax.slice_in_dim(cells, cells.shape[dim] - width, cells.shape[dim], axis=dim)
        cells = jnp.concatenate(
            [
                lax.ppermute(tail, axis, [(i, (i + 1) % count) for i in range(count)]),
                cells,
                lax.ppermute(head, axis, [((i + 1) % count, i) for i in range(count)]),
            ],
            axis=dim,
        )
    return cells


def diffuse(extended, diffusivity):
    middle = extended[1:-1]
    padded = jnp.pad(middle, ((0, 0), (1, 1), (0, 0), (0, 0)))
    laplace = extended[2:] + extended[:-2] + padded[:, 2:] + padded[:, :-2] - 4.0 * middle
    return middle + diffusivity * laplace


def smooth(profile, diffusivity):
    for repeat in range(NSTEP):
        extended = padded_2(profile, (("tile", 0),), 1)
        profile = diffuse(extended, diffusivity)
    return profile


def band_matrix(jacobian_rows, offset_rows):
    band_width = jacobian_rows.shape[-1]
    pad_spec = [(0, 0)] * (jacobian_rows.ndim - 1) + [(0, LEV - band_width)]
    widened = jnp.pad(jacobian_rows, pad_spec)
    bit_count = max((LEV - 1).bit_length(), 1)
    for bit_number in range(bit_count):
        step_size = 1 << bit_number
        moved = jnp.roll(widened, step_size, axis=-1)
        chosen = (offset_rows // step_size % 2 == 1)[..., None]
        widened = jnp.where(chosen, moved, widened)
    return widened


def respond(rows_in, dense_map, weights):
    brightness = lax.dot_general(
        rows_in, dense_map, (((1,), (1,)), ((), ())), preferred_element_type=jnp.float32
    )
    weighted = weights * brightness
    energy = jnp.sum(brightness * weighted, axis=1)
    adjoint = jnp.dot(weighted.astype(jnp.bfloat16), dense_map, preferred_element_type=jnp.float32)
    return (adjoint.astype(jnp.bfloat16), energy)


def body(probes, stddev, diffusivity, counts, columns, jacobian, offsets, obs_weights):
    tile_count = lax.axis_size("tile")
    my_section = lax.axis_index("tile")
    row_count, col_count, probe_count, levels = probes.shape
    slot_count = columns.shape[2]
    cell_count = row_count * col_count
    spread = stddev[:, :, None, :]
    profile = (spread * smooth(probes.astype(jnp.float32), diffusivity)).astype(jnp.bfloat16)
    flat_profile = profile.reshape(cell_count, probe_count, levels)
    targets = columns[0]
    live_slots = jnp.arange(slot_count, dtype=jnp.int32)[None, :] < counts[0][:, None]
    cell_ids = jnp.arange(cell_count, dtype=jnp.int32)
    selector = ((targets[:, :, None] == cell_ids[None, None, :]) & live_slots[:, :, None]).astype(
        jnp.bfloat16
    )
    outgoing = jnp.einsum(
        "tkn,npl->tkpl", selector, flat_profile, preferred_element_type=jnp.float32
    ).astype(jnp.bfloat16)
    own_offsets = lax.dynamic_index_in_dim(offsets, my_section, 0, keepdims=False)
    dense_map = band_matrix(jacobian[0], own_offsets)
    weights = lax.dynamic_index_in_dim(obs_weights, my_section, 0, keepdims=False)
    arrived = lax.all_to_all(outgoing, "tile", split_axis=0, concat_axis=0, tiled=True)
    sources, slot_here, probe_here, level_here = arrived.shape
    group_size = math.gcd(sources, 8)
    stacked = arrived.reshape(
        sources // group_size, group_size * slot_here * probe_here, level_here
    )

    def radiate(batch_rows):
        return respond(batch_rows, dense_map, weights)

    adjoint, energy = lax.map(radiate, stacked)
    energy = energy.reshape(sources, slot_here, probe_here).sum(axis=2)
    adjoints_here = adjoint.reshape(arrived.shape)
    returned = lax.all_to_all(adjoints_here, "tile", split_axis=0, concat_axis=0, tiled=True)
    section_part = jnp.sum(energy).reshape(1)
    totals = lax.psum(section_part, "lev")
    trace_share = totals * (1.0 / (PROBES * tile_count * slot_count * CH))
    gradient = jnp.einsum("tkn,tkpl->npl", selector, returned, preferred_element_type=jnp.float32)
    gradient = gradient.reshape(row_count, col_count, probe_count, levels)
    hessian = smooth(spread * gradient, diffusivity)
    return (hessian, trace_share)


def solution(mesh):
    placed = (
        P("tile", None, "lev", None),
        P("tile", None, None),
        P(),
        P("tile", None),
        P("tile", None, None),
        P("tile", None, None),
        P(),
        P(),
    )
    return jax.shard_map(
        body,
        mesh=mesh,
        in_specs=placed,
        out_specs=(P("tile", None, "lev", None), P("tile")),
        check_vma=False,
    )
```

profile of v0, /device:TPU:32, one launch (start us, length us, event | category | flops | bytes accessed | tf_op | source)
XLA Modules:
  0.0 203.5 jit_solution(3389362068707142357)
XLA Ops:
  0.7 0.8 fusion.54
  1.5 3.7 %collective-permute-start = (f32[1,32,2,128]{3,2,1,0:T(2,128)S(1)}, f32[1,32,2,128]{3,2,1,0:T(2,128)S(1)}, u32[]{:S(2)}, u32[]{:S(2)}) collective-permute-start(f32[1,32,2,128]{3,2,1,0:T(2,128)S(1)} %get-tuple-element.61), channel_id=1, source_target_pairs={{4,0},{8,4},{12,8},{16,12},{20,16},{24,20},{28,24},{32,28},{36,32}... | collective-permute-start | bytes 98312 | tf_op jit(solution)/shard_map/ppermute | solution.py:22
  5.1 1.9 collective-permute-start.1
  7.0 0.9 convert_element_type.23
  7.9 4.5 %collective-permute-done.1 = f32[1,32,2,128]{3,2,1,0:T(2,128)S(1)} collective-permute-done((f32[1,32,2,128]{3,2,1,0:T(2,128)S(1)}, f32[1,32,2,128]{3,2,1,0:T(2,128)S(1)}, u32[]{:S(2)}, u32[]{:S(2)}) %collective-permute-start.1) | collective-permute-done | bytes 32800 | tf_op jit(solution)/shard_map/ppermute | solution.py:20
  12.5 0.8 multiply_add_fusion.2
  13.3 1.9 collective-permute-start.2
  15.2 2.4 %collective-permute-start.3 = (f32[1,32,2,128]{3,2,1,0:T(2,128)S(1)}, f32[1,32,2,128]{3,2,1,0:T(2,128)S(1)}, u32[]{:S(2)}, u32[]{:S(2)}) collective-permute-start(f32[1,32,2,128]{3,2,1,0:T(2,128)S(1)} %get-tuple-element.58), channel_id=1, source_target_pairs={{0,4},{4,8},{8,12},{12,16},{16,20},{20,24},{24,28},{28,32},{32,36}... | collective-permute-start | bytes 98312 | tf_op jit(solution)/shard_map/ppermute | solution.py:20
  18.3 4.3 %collective-permute-done.3 = f32[1,32,2,128]{3,2,1,0:T(2,128)S(1)} collective-permute-done((f32[1,32,2,128]{3,2,1,0:T(2,128)S(1)}, f32[1,32,2,128]{3,2,1,0:T(2,128)S(1)}, u32[]{:S(2)}, u32[]{:S(2)}) %collective-permute-start.3) | collective-permute-done | bytes 32800 | tf_op jit(solution)/shard_map/ppermute | solution.py:20
  22.6 1.0 multiply_convert_fusion.2
  24.1 2.1 %copy.22 = bf16[128,16,2,128]{3,2,1,0:T(2,128)(2,1)} copy(bf16[128,16,2,128]{3,0,2,1:T(8,128)(2,1)S(1)} %convolution_convert_fusion.1) | data formatting | bytes 2097152 | tf_op jit(solution)/shard_map/convert_element_type | solution.py:83
  26.2 19.1 %all-to-all-start = ((bf16[128,16,2,128]{3,2,1,0:T(2,128)(2,1)}), bf16[128,16,2,128]{3,2,1,0:T(2,128)(2,1)S(1)}, u32[]{:S(2)}, u32[]{:S(2)}) async-start(bf16[128,16,2,128]{3,2,1,0:T(2,128)(2,1)} %copy.22), calls=%async_computation | async-start | bytes 2097152 | tf_op jit(solution)/shard_map/all_to_all | solution.py:87
  46.6 0.7 constant_dynamic-slice_fusion.1
  47.7 53.0 %all-to-all-done = bf16[128,16,2,128]{3,2,1,0:T(2,128)(2,1)S(1)} async-done(((bf16[128,16,2,128]{3,2,1,0:T(2,128)(2,1)}), bf16[128,16,2,128]{3,2,1,0:T(2,128)(2,1)S(1)}, u32[]{:S(2)}, u32[]{:S(2)}) %all-to-all-start) | async-done | bytes 1048608 | tf_op jit(solution)/shard_map/all_to_all | solution.py:87
  100.7 9.9 %while.12 = (s32[]{:T(128)}, bf16[16,256,128]{2,1,0:T(8,128)(2,1)S(1)}, f32[16,256]{1,0:T(8,128)S(1)}, f32[256]{0:T(256)S(1)}, bf16[16,256,128]{2,1,0:T(8,128)(2...) while((s32[]{:T(128)}, bf16[16,256,128]{2,1,0:T(8,128)(2,1)S(1)}, f32[16,256]{1,0:T(8,128)S(1)}, ...), condition=%wide.region_2.3_spmd, body=%wide.region_0.2_spmd.sunk | while | flops 33914624 | bytes 791657 | solution.py:97
  110.9 61.9 %all_to_all.10 = bf16[128,16,2,128]{3,1,2,0:T(8,128)(2,1)S(1)} all-to-all(bf16[128,16,2,128]{3,1,2,0:T(8,128)(2,1)S(1)} %copy.24), channel_id=1, replica_groups=mesh['tile'=128,'lev'=4] {'tile'}, dimensions={0} | all-to-all | bytes 2097152 | tf_op jit(solution)/shard_map/all_to_all | solution.py:100
  172.7 0.8 fusion.8
  173.7 3.4 %collective-permute-start.4 = (f32[1,32,2,128]{3,2,1,0:T(2,128)S(1)}, f32[1,32,2,128]{3,2,1,0:T(2,128)S(1)}, u32[]{:S(2)}, u32[]{:S(2)}) collective-permute-start(f32[1,32,2,128]{3,2,1,0:T(2,128)S(1)} %get-tuple-element.55), channel_id=1, source_target_pairs={{4,0},{8,4},{12,8},{16,12},{20,16},{24,20},{28,24},{32,28},{36,32}... | collective-permute-start | bytes 98312 | tf_op jit(solution)/shard_map/ppermute | solution.py:22
  177.1 1.9 collective-permute-start.5
  179.1 5.4 %collective-permute-done.5 = f32[1,32,2,128]{3,2,1,0:T(2,128)S(1)} collective-permute-done((f32[1,32,2,128]{3,2,1,0:T(2,128)S(1)}, f32[1,32,2,128]{3,2,1,0:T(2,128)S(1)}, u32[]{:S(2)}, u32[]{:S(2)}) %collective-permute-start.5) | collective-permute-done | bytes 32800 | tf_op jit(solution)/shard_map/ppermute | solution.py:20
  184.6 1.9 collective-permute-start.6
  186.6 2.4 %collective-permute-start.7 = (f32[1,32,2,128]{3,2,1,0:T(2,128)S(1)}, f32[1,32,2,128]{3,2,1,0:T(2,128)S(1)}, u32[]{:S(2)}, u32[]{:S(2)}) collective-permute-start(f32[1,32,2,128]{3,2,1,0:T(2,128)S(1)} %get-tuple-element.54), channel_id=1, source_target_pairs={{0,4},{4,8},{8,12},{12,16},{16,20},{20,24},{24,28},{28,32},{32,36}... | collective-permute-start | bytes 98312 | tf_op jit(solution)/shard_map/ppermute | solution.py:20
  189.6 11.3 %psum.7 = f32[1]{0:T(128)} all-reduce(f32[1]{0:T(128)} %bitcast.17), channel_id=1, replica_groups=mesh['tile'=128,'lev'=4] {'lev'}, use_global_device_ids=true, to_apply=%region_4.5 | all-reduce | flops 1 | bytes 8 | tf_op jit(solution)/shard_map/psum | solution.py:102
  201.6 0.8 multiply_add_fusion
  (92 shorter events, 13.4 us)
Async XLA Ops:
  0.6 44.8 %copy-start = (s32[128,256]{1,0:T(8,128)S(1)}, s32[128,256]{1,0:T(8,128)}, u32[]{:S(2)}) copy-start(s32[128,256]{1,0:T(8,128)} %param.16) | copy-start | bytes 393220
  0.6 23.0 %copy-start.3 = (s32[1,128,16]{1,2,0:T(8,128)S(1)}, s32[1,128,16]{1,2,0:T(8,128)}, u32[]{:S(2)}) copy-start(s32[1,128,16]{1,2,0:T(8,128)} %param.14) | copy-start | bytes 24580
  1.5 6.5 %collective-permute-start = (f32[1,32,2,128]{3,2,1,0:T(2,128)S(1)}, f32[1,32,2,128]{3,2,1,0:T(2,128)S(1)}, u32[]{:S(2)}, u32[]{:S(2)}) collective-permute-start(f32[1,32,2,128]{3,2,1,0:T(2,128)S(1)} %get-tuple-element.61), channel_id=1, source_target_pairs={{4,0},{8,4},{12,8},{16,12},{20,16},{24,20},{28,24},{32,28},{36,32}... | collective-permute-start | bytes 98312 | tf_op jit(solution)/shard_map/ppermute | solution.py:22
  5.1 7.3 %collective-permute-start.1 = (f32[1,32,2,128]{3,2,1,0:T(2,128)S(1)}, f32[1,32,2,128]{3,2,1,0:T(2,128)S(1)}, u32[]{:S(2)}, u32[]{:S(2)}) collective-permute-start(f32[1,32,2,128]{3,2,1,0:T(2,128)S(1)} %get-tuple-element.62), channel_id=1, source_target_pairs={{0,4},{4,8},{8,12},{12,16},{16,20},{20,24},{24,28},{28,32},{32,36}... | collective-permute-start | bytes 98312 | tf_op jit(solution)/shard_map/ppermute | solution.py:20
  13.3 5.0 %collective-permute-start.2 = (f32[1,32,2,128]{3,2,1,0:T(2,128)S(1)}, f32[1,32,2,128]{3,2,1,0:T(2,128)S(1)}, u32[]{:S(2)}, u32[]{:S(2)}) collective-permute-start(f32[1,32,2,128]{3,2,1,0:T(2,128)S(1)} %get-tuple-element.57), channel_id=1, source_target_pairs={{4,0},{8,4},{12,8},{16,12},{20,16},{24,20},{28,24},{32,28},{36,32}... | collective-permute-start | bytes 98312 | tf_op jit(solution)/shard_map/ppermute | solution.py:22
  15.2 7.3 %collective-permute-start.3 = (f32[1,32,2,128]{3,2,1,0:T(2,128)S(1)}, f32[1,32,2,128]{3,2,1,0:T(2,128)S(1)}, u32[]{:S(2)}, u32[]{:S(2)}) collective-permute-start(f32[1,32,2,128]{3,2,1,0:T(2,128)S(1)} %get-tuple-element.58), channel_id=1, source_target_pairs={{0,4},{4,8},{8,12},{12,16},{16,20},{20,24},{24,28},{28,32},{32,36}... | collective-permute-start | bytes 98312 | tf_op jit(solution)/shard_map/ppermute | solution.py:20
  26.2 19.1 %copy-start.2 = (bf16[1,256,32]{1,2,0:T(8,128)(2,1)S(1)}, bf16[1,256,32]{1,2,0:T(8,128)(2,1)}, u32[]{:S(2)}) copy-start(bf16[1,256,32]{1,2,0:T(8,128)(2,1)} %param.15) | copy-start | bytes 49156
  26.2 74.6 %all-to-all-start = ((bf16[128,16,2,128]{3,2,1,0:T(2,128)(2,1)}), bf16[128,16,2,128]{3,2,1,0:T(2,128)(2,1)S(1)}, u32[]{:S(2)}, u32[]{:S(2)}) async-start(bf16[128,16,2,128]{3,2,1,0:T(2,128)(2,1)} %copy.22), calls=%async_computation | async-start | bytes 2097152 | tf_op jit(solution)/shard_map/all_to_all | solution.py:87
  172.7 0.8 copy-start.1
  172.7 11.7 %copy-start.4 = (f32[128]{0:T(128)S(1)}, f32[128]{0:T(128)}, u32[]{:S(2)}) copy-start(f32[128]{0:T(128)} %param.12) | copy-start | bytes 1540
  173.7 5.3 %collective-permute-start.4 = (f32[1,32,2,128]{3,2,1,0:T(2,128)S(1)}, f32[1,32,2,128]{3,2,1,0:T(2,128)S(1)}, u32[]{:S(2)}, u32[]{:S(2)}) collective-permute-start(f32[1,32,2,128]{3,2,1,0:T(2,128)S(1)} %get-tuple-element.55), channel_id=1, source_target_pairs={{4,0},{8,4},{12,8},{16,12},{20,16},{24,20},{28,24},{32,28},{36,32}... | collective-permute-start | bytes 98312 | tf_op jit(solution)/shard_map/ppermute | solution.py:22
  177.1 7.3 %collective-permute-start.5 = (f32[1,32,2,128]{3,2,1,0:T(2,128)S(1)}, f32[1,32,2,128]{3,2,1,0:T(2,128)S(1)}, u32[]{:S(2)}, u32[]{:S(2)}) collective-permute-start(f32[1,32,2,128]{3,2,1,0:T(2,128)S(1)} %get-tuple-element.56), channel_id=1, source_target_pairs={{0,4},{4,8},{8,12},{12,16},{16,20},{20,24},{24,28},{28,32},{32,36}... | collective-permute-start | bytes 98312 | tf_op jit(solution)/shard_map/ppermute | solution.py:20
  184.6 17.0 %collective-permute-start.6 = (f32[1,32,2,128]{3,2,1,0:T(2,128)S(1)}, f32[1,32,2,128]{3,2,1,0:T(2,128)S(1)}, u32[]{:S(2)}, u32[]{:S(2)}) collective-permute-start(f32[1,32,2,128]{3,2,1,0:T(2,128)S(1)} %get-tuple-element.53), channel_id=1, source_target_pairs={{4,0},{8,4},{12,8},{16,12},{20,16},{24,20},{28,24},{32,28},{36,32}... | collective-permute-start | bytes 98312 | tf_op jit(solution)/shard_map/ppermute | solution.py:22
  186.6 15.0 %collective-permute-start.7 = (f32[1,32,2,128]{3,2,1,0:T(2,128)S(1)}, f32[1,32,2,128]{3,2,1,0:T(2,128)S(1)}, u32[]{:S(2)}, u32[]{:S(2)}) collective-permute-start(f32[1,32,2,128]{3,2,1,0:T(2,128)S(1)} %get-tuple-element.54), channel_id=1, source_target_pairs={{0,4},{4,8},{8,12},{12,16},{16,20},{20,24},{24,28},{28,32},{32,36}... | collective-permute-start | bytes 98312 | tf_op jit(solution)/shard_map/ppermute | solution.py:20
where the time goes:
time: 204 us
  blocking collectives  73.2 us (36%)
  waiting for transfers between devices  67.2 us (33%)
  starting transfers between devices  38.6 us (19%)
  matrix products  10.1 us (5%)
  other arithmetic  5.97 us (3%)
  local copies, waits for them, and re-layouts  5.19 us (3%)
  between operations  2.76 us (1%)
    all_to_all x1, blocking collectives, body(): lax.all_to_all(adjoints_here, 'tile', split_axis=0, concat_axis=0, tiled=...  61.9 us
    all_to_all x1, waiting for transfers between devices, body(): lax.all_to_all(outgoing, 'tile', split_axis=0, concat_axis=0, tiled=True)  53 us
    all_to_all x1, starting transfers between devices, body(): lax.all_to_all(outgoing, 'tile', split_axis=0, concat_axis=0, tiled=True)  19.1 us
    ppermute x4, waiting for transfers between devices, padded_2(): lax.ppermute(tail, axis, [(i, (i + 1) % count) for i in range(count)])  14.2 us
    psum x1, blocking collectives, body(): totals = lax.psum(section_part, 'lev')  11.3 us
    ppermute x4, starting transfers between devices, padded_2(): lax.ppermute(head, axis, [((i + 1) % count, i) for i in range(count)])  10.9 us
    ppermute x4, starting transfers between devices, padded_2(): lax.ppermute(tail, axis, [(i, (i + 1) % count) for i in range(count)])  8.65 us
    dot_general x16, matrix products, respond(): jnp.dot(weighted.astype(jnp.bfloat16), dense_map, preferred_element_type=...  5.18 us
  transfers between devices with their start and end apart: 9, of which 4 were waited for; matrix products, arithmetic and copies ran while one was open for 2% of the time, Pallas kernels for 0%

commit v1 on v0

--- a/solution.py
+++ b/solution.py
@@ -64,6 +64,18 @@
 
 
 def body(probes, stddev, diffusivity, counts, columns, jacobian, offsets, obs_weights):
+
+    def raise_slices_on_mesh(slab_in):
+        total_devices = lax.psum(1, "lev")
+        formed, block_last = (slab_in, 0)
+        while 1 << block_last < total_devices:
+            block_next = lax.ppermute(
+                formed, "lev", tuple(((num, num ^ 1 << block_last) for num in range(total_devices)))
+            )
+            formed = formed + block_next
+            block_last = block_last + 1
+        return formed
+
     tile_count = lax.axis_size("tile")
     my_section = lax.axis_index("tile")
     row_count, col_count, probe_count, levels = probes.shape
@@ -99,7 +111,7 @@
     adjoints_here = adjoint.reshape(arrived.shape)
     returned = lax.all_to_all(adjoints_here, "tile", split_axis=0, concat_axis=0, tiled=True)
     section_part = jnp.sum(energy).reshape(1)
-    totals = lax.psum(section_part, "lev")
+    totals = raise_slices_on_mesh(section_part)
     trace_share = totals * (1.0 / (PROBES * tile_count * slot_count * CH))
     gradient = jnp.einsum("tkn,tkpl->npl", selector, returned, preferred_element_type=jnp.float32)
     gradient = gradient.reshape(row_count, col_count, probe_count, levels)

time: 204 us -> 207 us (1.015)
  the two profiles are of different devices: /device:TPU:32 before, /device:TPU:56 now
where the time goes in v1:
time: 207 us; the launch traced here: 206 us
  waiting for transfers between devices  72.9 us (35%)
  blocking collectives  61.9 us (30%)
  starting transfers between devices  45.7 us (22%)
  matrix products  10.1 us (5%)
  other arithmetic  5.97 us (3%)
  local copies, waits for them, and re-layouts  5.2 us (3%)
  between operations  3.89 us (2%)
    all_to_all x1, blocking collectives, body(): lax.all_to_all(adjoints_here, 'tile', split_axis=0, concat_axis=0, tiled=...  61.9 us
    all_to_all x1, waiting for transfers between devices, body(): lax.all_to_all(outgoing, 'tile', split_axis=0, concat_axis=0, tiled=True)  53 us
    all_to_all x1, starting transfers between devices, body(): lax.all_to_all(outgoing, 'tile', split_axis=0, concat_axis=0, tiled=True)  19.1 us
    ppermute x4, waiting for transfers between devices, padded_2(): lax.ppermute(tail, axis, [(i, (i + 1) % count) for i in range(count)])  14.2 us
    ppermute x4, starting transfers between devices, padded_2(): lax.ppermute(head, axis, [((i + 1) % count, i) for i in range(count)])  10.9 us
    ppermute x4, starting transfers between devices, padded_2(): lax.ppermute(tail, axis, [(i, (i + 1) % count) for i in range(count)])  8.65 us
    ppermute x2, starting transfers between devices, raise_slices_on_mesh(): lax.ppermute(formed, 'lev', tuple(((num, num ^ 1 << block_last) for num i...  7.06 us
    ppermute x2, waiting for transfers between devices, raise_slices_on_mesh(): lax.ppermute(formed, 'lev', tuple(((num, num ^ 1 << block_last) for num i...  5.64 us
  transfers between devices with their start and end apart: 11, of which 6 were waited for; matrix products, arithmetic and copies ran while one was open for 2% of the time, Pallas kernels for 0%

profile of v1, /device:TPU:56, one launch (start us, length us, event | category | flops | bytes accessed | tf_op | source)
XLA Modules:
  0.0 206.0 jit_solution(5120154758857040624)
XLA Ops:
  1.5 3.7 %collective-permute-start = (f32[1,32,2,128]{3,2,1,0:T(2,128)S(1)}, f32[1,32,2,128]{3,2,1,0:T(2,128)S(1)}, u32[]{:S(2)}, u32[]{:S(2)}) collective-permute-start(f32[1,32,2,128]{3,2,1,0:T(2,128)S(1)} %get-tuple-element.61), channel_id=1, source_target_pairs={{4,0},{8,4},{12,8},{16,12},{20,16},{24,20},{28,24},{32,28},{36,32}... | collective-permute-start | bytes 98312 | tf_op jit(solution)/shard_map/ppermute | solution.py:22
  5.1 1.9 collective-permute-start.1
  7.0 0.9 convert_element_type.23
  7.9 4.5 %collective-permute-done.1 = f32[1,32,2,128]{3,2,1,0:T(2,128)S(1)} collective-permute-done((f32[1,32,2,128]{3,2,1,0:T(2,128)S(1)}, f32[1,32,2,128]{3,2,1,0:T(2,128)S(1)}, u32[]{:S(2)}, u32[]{:S(2)}) %collective-permute-start.1) | collective-permute-done | bytes 32800 | tf_op jit(solution)/shard_map/ppermute | solution.py:20
  12.5 0.8 multiply_add_fusion.2
  13.3 1.9 collective-permute-start.2
  15.2 2.4 %collective-permute-start.3 = (f32[1,32,2,128]{3,2,1,0:T(2,128)S(1)}, f32[1,32,2,128]{3,2,1,0:T(2,128)S(1)}, u32[]{:S(2)}, u32[]{:S(2)}) collective-permute-start(f32[1,32,2,128]{3,2,1,0:T(2,128)S(1)} %get-tuple-element.58), channel_id=1, source_target_pairs={{0,4},{4,8},{8,12},{12,16},{16,20},{20,24},{24,28},{28,32},{32,36}... | collective-permute-start | bytes 98312 | tf_op jit(solution)/shard_map/ppermute | solution.py:20
  18.3 4.3 %collective-permute-done.3 = f32[1,32,2,128]{3,2,1,0:T(2,128)S(1)} collective-permute-done((f32[1,32,2,128]{3,2,1,0:T(2,128)S(1)}, f32[1,32,2,128]{3,2,1,0:T(2,128)S(1)}, u32[]{:S(2)}, u32[]{:S(2)}) %collective-permute-start.3) | collective-permute-done | bytes 32800 | tf_op jit(solution)/shard_map/ppermute | solution.py:20
  22.6 1.0 multiply_convert_fusion.2
  24.1 2.1 %copy.22 = bf16[128,16,2,128]{3,2,1,0:T(2,128)(2,1)} copy(bf16[128,16,2,128]{3,0,2,1:T(8,128)(2,1)S(1)} %convolution_convert_fusion.1) | data formatting | bytes 2097152 | tf_op jit(solution)/shard_map/convert_element_type | solution.py:95
  26.2 19.1 %all-to-all-start = ((bf16[128,16,2,128]{3,2,1,0:T(2,128)(2,1)}), bf16[128,16,2,128]{3,2,1,0:T(2,128)(2,1)S(1)}, u32[]{:S(2)}, u32[]{:S(2)}) async-start(bf16[128,16,2,128]{3,2,1,0:T(2,128)(2,1)} %copy.22), calls=%async_computation | async-start | bytes 2097152 | tf_op jit(solution)/shard_map/all_to_all | solution.py:99
  47.7 53.0 %all-to-all-done = bf16[128,16,2,128]{3,2,1,0:T(2,128)(2,1)S(1)} async-done(((bf16[128,16,2,128]{3,2,1,0:T(2,128)(2,1)}), bf16[128,16,2,128]{3,2,1,0:T(2,128)(2,1)S(1)}, u32[]{:S(2)}, u32[]{:S(2)}) %all-to-all-start) | async-done | bytes 1048608 | tf_op jit(solution)/shard_map/all_to_all | solution.py:99
  100.7 9.9 %while.12 = (s32[]{:T(128)}, bf16[16,256,128]{2,1,0:T(8,128)(2,1)S(1)}, f32[16,256]{1,0:T(8,128)S(1)}, f32[256]{0:T(256)S(1)}, bf16[16,256,128]{2,1,0:T(8,128)(2...) while((s32[]{:T(128)}, bf16[16,256,128]{2,1,0:T(8,128)(2,1)S(1)}, f32[16,256]{1,0:T(8,128)S(1)}, ...), condition=%wide.region_2.3_spmd, body=%wide.region_0.2_spmd.sunk | while | flops 33914624 | bytes 791657 | solution.py:109
  110.9 61.9 %all_to_all.10 = bf16[128,16,2,128]{3,1,2,0:T(8,128)(2,1)S(1)} all-to-all(bf16[128,16,2,128]{3,1,2,0:T(8,128)(2,1)S(1)} %copy.24), channel_id=1, replica_groups=mesh['tile'=128,'lev'=4] {'tile'}, dimensions={0} | all-to-all | bytes 2097152 | tf_op jit(solution)/shard_map/all_to_all | solution.py:112
  173.7 3.4 %collective-permute-start.4 = (f32[1,32,2,128]{3,2,1,0:T(2,128)S(1)}, f32[1,32,2,128]{3,2,1,0:T(2,128)S(1)}, u32[]{:S(2)}, u32[]{:S(2)}) collective-permute-start(f32[1,32,2,128]{3,2,1,0:T(2,128)S(1)} %get-tuple-element.55), channel_id=1, source_target_pairs={{4,0},{8,4},{12,8},{16,12},{20,16},{24,20},{28,24},{32,28},{36,32}... | collective-permute-start | bytes 98312 | tf_op jit(solution)/shard_map/ppermute | solution.py:22
  177.1 1.9 collective-permute-start.5
  179.1 5.4 %collective-permute-done.5 = f32[1,32,2,128]{3,2,1,0:T(2,128)S(1)} collective-permute-done((f32[1,32,2,128]{3,2,1,0:T(2,128)S(1)}, f32[1,32,2,128]{3,2,1,0:T(2,128)S(1)}, u32[]{:S(2)}, u32[]{:S(2)}) %collective-permute-start.5) | collective-permute-done | bytes 32800 | tf_op jit(solution)/shard_map/ppermute | solution.py:20
  184.6 1.9 collective-permute-start.6
  186.6 2.4 %collective-permute-start.7 = (f32[1,32,2,128]{3,2,1,0:T(2,128)S(1)}, f32[1,32,2,128]{3,2,1,0:T(2,128)S(1)}, u32[]{:S(2)}, u32[]{:S(2)}) collective-permute-start(f32[1,32,2,128]{3,2,1,0:T(2,128)S(1)} %get-tuple-element.54), channel_id=1, source_target_pairs={{0,4},{4,8},{8,12},{12,16},{16,20},{20,24},{24,28},{28,32},{32,36}... | collective-permute-start | bytes 98312 | tf_op jit(solution)/shard_map/ppermute | solution.py:20
  189.6 2.6 %collective-permute-start.8 = (f32[1]{0:T(128)}, f32[1]{0:T(128)}, u32[]{:S(2)}, u32[]{:S(2)}) collective-permute-start(f32[1]{0:T(128)} %bitcast.17), channel_id=1, source_target_pairs={{0,1},{1,0},{2,3},{3,2},{4,5},{5,4},{6,7},{7,6},{8,9},{9,8},{10,11... | collective-permute-start | bytes 20 | tf_op jit(solution)/shard_map/ppermute | solution.py:72
  192.2 3.0 %collective-permute-done.8 = f32[1]{0:T(128)} collective-permute-done((f32[1]{0:T(128)}, f32[1]{0:T(128)}, u32[]{:S(2)}, u32[]{:S(2)}) %collective-permute-start.8) | collective-permute-done | bytes 36 | tf_op jit(solution)/shard_map/ppermute | solution.py:72
  196.5 4.4 %collective-permute-start.9 = (f32[1]{0:T(128)}, f32[1]{0:T(128)}, u32[]{:S(2)}, u32[]{:S(2)}) collective-permute-start(f32[1]{0:T(128)} %add.189), channel_id=1, source_target_pairs={{0,2},{1,3},{2,0},{3,1},{4,6},{5,7},{6,4},{7,5},{8,10},{9,11},{10,... | collective-permute-start | bytes 20 | tf_op jit(solution)/shard_map/ppermute | solution.py:72
  200.9 2.6 %collective-permute-done.9 = f32[1]{0:T(128)} collective-permute-done((f32[1]{0:T(128)}, f32[1]{0:T(128)}, u32[]{:S(2)}, u32[]{:S(2)}) %collective-permute-start.9) | collective-permute-done | bytes 36 | tf_op jit(solution)/shard_map/ppermute | solution.py:72
  204.1 0.8 multiply_add_fusion
  (95 shorter events, 15.7 us)
Async XLA Ops:
  0.6 44.8 %copy-start = (s32[128,256]{1,0:T(8,128)S(1)}, s32[128,256]{1,0:T(8,128)}, u32[]{:S(2)}) copy-start(s32[128,256]{1,0:T(8,128)} %param.16) | copy-start | bytes 393220
  0.6 23.0 %copy-start.3 = (s32[1,128,16]{1,2,0:T(8,128)S(1)}, s32[1,128,16]{1,2,0:T(8,128)}, u32[]{:S(2)}) copy-start(s32[1,128,16]{1,2,0:T(8,128)} %param.14) | copy-start | bytes 24580
  1.5 6.5 %collective-permute-start = (f32[1,32,2,128]{3,2,1,0:T(2,128)S(1)}, f32[1,32,2,128]{3,2,1,0:T(2,128)S(1)}, u32[]{:S(2)}, u32[]{:S(2)}) collective-permute-start(f32[1,32,2,128]{3,2,1,0:T(2,128)S(1)} %get-tuple-element.61), channel_id=1, source_target_pairs={{4,0},{8,4},{12,8},{16,12},{20,16},{24,20},{28,24},{32,28},{36,32}... | collective-permute-start | bytes 98312 | tf_op jit(solution)/shard_map/ppermute | solution.py:22
  5.1 7.3 %collective-permute-start.1 = (f32[1,32,2,128]{3,2,1,0:T(2,128)S(1)}, f32[1,32,2,128]{3,2,1,0:T(2,128)S(1)}, u32[]{:S(2)}, u32[]{:S(2)}) collective-permute-start(f32[1,32,2,128]{3,2,1,0:T(2,128)S(1)} %get-tuple-element.62), channel_id=1, source_target_pairs={{0,4},{4,8},{8,12},{12,16},{16,20},{20,24},{24,28},{28,32},{32,36}... | collective-permute-start | bytes 98312 | tf_op jit(solution)/shard_map/ppermute | solution.py:20
  13.3 5.0 %collective-permute-start.2 = (f32[1,32,2,128]{3,2,1,0:T(2,128)S(1)}, f32[1,32,2,128]{3,2,1,0:T(2,128)S(1)}, u32[]{:S(2)}, u32[]{:S(2)}) collective-permute-start(f32[1,32,2,128]{3,2,1,0:T(2,128)S(1)} %get-tuple-element.57), channel_id=1, source_target_pairs={{4,0},{8,4},{12,8},{16,12},{20,16},{24,20},{28,24},{32,28},{36,32}... | collective-permute-start | bytes 98312 | tf_op jit(solution)/shard_map/ppermute | solution.py:22
  15.2 7.3 %collective-permute-start.3 = (f32[1,32,2,128]{3,2,1,0:T(2,128)S(1)}, f32[1,32,2,128]{3,2,1,0:T(2,128)S(1)}, u32[]{:S(2)}, u32[]{:S(2)}) collective-permute-start(f32[1,32,2,128]{3,2,1,0:T(2,128)S(1)} %get-tuple-element.58), channel_id=1, source_target_pairs={{0,4},{4,8},{8,12},{12,16},{16,20},{20,24},{24,28},{28,32},{32,36}... | collective-permute-start | bytes 98312 | tf_op jit(solution)/shard_map/ppermute | solution.py:20
  26.2 19.1 %copy-start.2 = (bf16[1,256,32]{1,2,0:T(8,128)(2,1)S(1)}, bf16[1,256,32]{1,2,0:T(8,128)(2,1)}, u32[]{:S(2)}) copy-start(bf16[1,256,32]{1,2,0:T(8,128)(2,1)} %param.15) | copy-start | bytes 49156
  26.2 74.6 %all-to-all-start = ((bf16[128,16,2,128]{3,2,1,0:T(2,128)(2,1)}), bf16[128,16,2,128]{3,2,1,0:T(2,128)(2,1)S(1)}, u32[]{:S(2)}, u32[]{:S(2)}) async-start(bf16[128,16,2,128]{3,2,1,0:T(2,128)(2,1)} %copy.22), calls=%async_computation | async-start | bytes 2097152 | tf_op jit(solution)/shard_map/all_to_all | solution.py:99
  172.7 0.8 copy-start.1
  172.7 11.7 %copy-start.4 = (f32[128]{0:T(128)S(1)}, f32[128]{0:T(128)}, u32[]{:S(2)}) copy-start(f32[128]{0:T(128)} %param.12) | copy-start | bytes 1540
  173.7 5.3 %collective-permute-start.4 = (f32[1,32,2,128]{3,2,1,0:T(2,128)S(1)}, f32[1,32,2,128]{3,2,1,0:T(2,128)S(1)}, u32[]{:S(2)}, u32[]{:S(2)}) collective-permute-start(f32[1,32,2,128]{3,2,1,0:T(2,128)S(1)} %get-tuple-element.55), channel_id=1, source_target_pairs={{4,0},{8,4},{12,8},{16,12},{20,16},{24,20},{28,24},{32,28},{36,32}... | collective-permute-start | bytes 98312 | tf_op jit(solution)/shard_map/ppermute | solution.py:22
  177.1 7.3 %collective-permute-start.5 = (f32[1,32,2,128]{3,2,1,0:T(2,128)S(1)}, f32[1,32,2,128]{3,2,1,0:T(2,128)S(1)}, u32[]{:S(2)}, u32[]{:S(2)}) collective-permute-start(f32[1,32,2,128]{3,2,1,0:T(2,128)S(1)} %get-tuple-element.56), channel_id=1, source_target_pairs={{0,4},{4,8},{8,12},{12,16},{16,20},{20,24},{24,28},{28,32},{32,36}... | collective-permute-start | bytes 98312 | tf_op jit(solution)/shard_map/ppermute | solution.py:20
  184.6 19.4 %collective-permute-start.6 = (f32[1,32,2,128]{3,2,1,0:T(2,128)S(1)}, f32[1,32,2,128]{3,2,1,0:T(2,128)S(1)}, u32[]{:S(2)}, u32[]{:S(2)}) collective-permute-start(f32[1,32,2,128]{3,2,1,0:T(2,128)S(1)} %get-tuple-element.53), channel_id=1, source_target_pairs={{4,0},{8,4},{12,8},{16,12},{20,16},{24,20},{28,24},{32,28},{36,32}... | collective-permute-start | bytes 98312 | tf_op jit(solution)/shard_map/ppermute | solution.py:22
  186.6 17.5 %collective-permute-start.7 = (f32[1,32,2,128]{3,2,1,0:T(2,128)S(1)}, f32[1,32,2,128]{3,2,1,0:T(2,128)S(1)}, u32[]{:S(2)}, u32[]{:S(2)}) collective-permute-start(f32[1,32,2,128]{3,2,1,0:T(2,128)S(1)} %get-tuple-element.54), channel_id=1, source_target_pairs={{0,4},{4,8},{8,12},{12,16},{16,20},{20,24},{24,28},{28,32},{32,36}... | collective-permute-start | bytes 98312 | tf_op jit(solution)/shard_map/ppermute | solution.py:20
  189.6 5.7 %collective-permute-start.8 = (f32[1]{0:T(128)}, f32[1]{0:T(128)}, u32[]{:S(2)}, u32[]{:S(2)}) collective-permute-start(f32[1]{0:T(128)} %bitcast.17), channel_id=1, source_target_pairs={{0,1},{1,0},{2,3},{3,2},{4,5},{5,4},{6,7},{7,6},{8,9},{9,8},{10,11... | collective-permute-start | bytes 20 | tf_op jit(solution)/shard_map/ppermute | solution.py:72
  196.5 7.0 %collective-permute-start.9 = (f32[1]{0:T(128)}, f32[1]{0:T(128)}, u32[]{:S(2)}, u32[]{:S(2)}) collective-permute-start(f32[1]{0:T(128)} %add.189), channel_id=1, source_target_pairs={{0,2},{1,3},{2,0},{3,1},{4,6},{5,7},{6,4},{7,5},{8,10},{9,11},{10,... | collective-permute-start | bytes 20 | tf_op jit(solution)/shard_map/ppermute | solution.py:72
